TPU v7x, 512 devices: a whole 4x8x8 slice. The times are simulated.
512 devices in a mesh: seq: 64 (over x, z, core), head: 8 (over y).
Axes of the slice: x: 4, y: 8, z: 8, core: 2. Of those that a mesh axis runs over, the one named last changes fastest.
Arguments:
- queries: bfloat16 [16384, 4096], P('seq', 'head'), may hold values from -6 to 6
- keys: bfloat16 [16384, 4096], P('seq', 'head'), may hold values from -6 to 6
- values: bfloat16 [16384, 4096], P('seq', 'head'), may hold values from -6 to 6
- gate: bfloat16 [16384, 4096], P('seq', 'head'), may hold values from -6 to 6
- residual: bfloat16 [16384, 4096], P('seq', 'head'), may hold values from -40 to 40
- log_decay: float32 [16384, 32], P('seq', 'head'), may hold values from -1 to 0, as said below
- out_weight: bfloat16 [4096, 4096], P('seq', 'head'), may hold values from -0.09375 to 0.09375
- norm_gain: bfloat16 [4096], P('head'), may hold values from 0.099609375 to 1.8984375
- kv_weight: bfloat16 [4096, 2048], P('seq', 'head'), may hold values from -0.09375 to 0.09375
Outputs:
- cache_keys: bfloat16 [16384, 1024], P('seq', 'head')
- cache_values: bfloat16 [16384, 1024], P('seq', 'head')
Inputs may be any that keep to these rules, and one draw needn't show every extreme that they name: `log_decay`: every entry is negative.
All inputs are finite; a program needn't handle non-finite values.
Results may differ from a plain program's by a relative error of at most 0.015.
Values may be sent and summed in bfloat16 or wider, within the bound.
A program may use at most 64 MiB of HBM per device.

v0:
```python
import jax
import jax.numpy as jnp
from jax import lax
from jax.sharding import PartitionSpec as P

HIGHEST = lax.Precision.HIGHEST


def entering(part, axis, combine, identity):
    place = lax.axis_index(axis)
    gathered = jax.tree.map(lambda a: lax.all_gather(a, axis), part)
    state = jax.tree.map(lambda a, e: jnp.zeros_like(a) + jnp.asarray(e, a.dtype), part, identity)

    def one(step, state):
        return combine(
            state, jax.tree.map(lambda a: lax.dynamic_index_in_dim(a, step, 0, False), gathered)
        )

    return lax.fori_loop(0, place, one, state)


def local_retention(queries, keys, values, log_decay, block):
    tokens, heads, width = queries.shape
    count = tokens // block

    def to_blocks(array):
        return array.reshape((count, block) + array.shape[1:])

    lower = jnp.arange(block)[:, None] >= jnp.arange(block)[None, :]

    def advance(carry, inputs):
        state, offset = carry
        query_block, key_block, value_block, decay_block = inputs
        within = jnp.cumsum(decay_block, axis=0)
        spread = within[:, None, :] - within[None, :, :]
        factor = jnp.where(
            lower[:, :, None], jnp.exp(jnp.where(lower[:, :, None], spread, 0.0)), 0.0
        )
        scores = jnp.einsum(
            "ihd,jhd->hij", query_block, key_block, preferred_element_type=jnp.float32
        )
        weighted = scores * jnp.transpose(factor, (2, 0, 1))
        values_wide = value_block.astype(jnp.float32)
        intra = jnp.einsum("hij,jhd->ihd", weighted, values_wide, precision=HIGHEST)
        query_wide = query_block.astype(jnp.float32)
        carried = jnp.exp(within)[:, :, None] * jnp.einsum(
            "ihd,hde->ihe", query_wide, state, precision=HIGHEST
        )
        ending = within[-1]
        key_wide = key_block.astype(jnp.float32) * jnp.exp(ending[None, :] - within)[:, :, None]
        fresh = jnp.exp(ending)[:, None, None] * state + jnp.einsum(
            "jhd,jhe->hde", key_wide, values_wide, precision=HIGHEST
        )
        return ((fresh, offset + ending), (intra + carried, offset[None, :] + within))

    start = (jnp.zeros((heads, width, width), jnp.float32), jnp.zeros((heads,), jnp.float32))
    final, stacked = lax.scan(
        advance,
        start,
        (to_blocks(queries), to_blocks(keys), to_blocks(values), to_blocks(log_decay)),
    )
    return (
        stacked[0].reshape(tokens, heads, width),
        stacked[1].reshape(tokens, heads),
        final[0],
        final[1],
    )


def combine_states(earlier, later):
    return (earlier[0] * later[0], later[0][:, None, None] * earlier[1] + later[1])


def on_device(queries, keys, values, gate, residual, log_decay, out_weight, norm_gain, kv_weight):
    tokens = queries.shape[0]
    heads = log_decay.shape[1]
    width = queries.shape[1] // heads
    shaped = [array.reshape(tokens, heads, width) for array in (queries, keys, values)]
    partial_out, running, state, offset = local_retention(
        shaped[0], shaped[1], shaped[2], log_decay, min(512, tokens)
    )
    identity = (jnp.ones((heads,), jnp.float32), jnp.zeros((heads, width, width), jnp.float32))
    scan_decay, incoming = entering((jnp.exp(offset), state), "seq", combine_states, identity)
    retained = partial_out + jnp.exp(running)[:, :, None] * jnp.einsum(
        "thd,hde->the", shaped[0].astype(jnp.float32), incoming, precision=HIGHEST
    )
    scale = lax.rsqrt(jnp.mean(retained * retained, axis=2, keepdims=True) + 1e-06)
    mixed = (
        jax.nn.silu(gate.astype(jnp.float32)) * (retained * scale).reshape(tokens, heads * width)
    ).astype(jnp.bfloat16)
    all_heads = lax.all_gather(mixed, "head", axis=1, tiled=True)
    out_full, kv_full = (
        lax.all_gather(out_weight, "seq", axis=0, tiled=True),
        lax.all_gather(kv_weight, "seq", axis=0, tiled=True),
    )
    branch = jnp.dot(all_heads, out_full, preferred_element_type=jnp.float32)
    hidden = (residual.astype(jnp.float32) + branch).astype(jnp.bfloat16)
    wide = hidden.astype(jnp.float32)
    squares = lax.psum(jnp.sum(wide * wide, axis=1), "head")
    features = wide.shape[1] * lax.axis_size("head")
    inverse = lax.rsqrt(squares[:, None] / features + 1e-06)
    local_norm = (wide * inverse * norm_gain.astype(jnp.float32)[None, :]).astype(jnp.bfloat16)
    normalized = lax.all_gather(local_norm, "head", axis=1, tiled=True)
    projected = jnp.dot(normalized, kv_full, preferred_element_type=jnp.float32)
    cache_heads = kv_weight.shape[1] // (2 * width)
    arranged = projected.reshape(tokens, cache_heads, 2, width)
    cache_keys = arranged[:, :, 0, :].reshape(tokens, cache_heads * width).astype(jnp.bfloat16)
    cache_values = arranged[:, :, 1, :].reshape(tokens, cache_heads * width).astype(jnp.bfloat16)
    return (cache_keys, cache_values)


def solution(mesh):
    placed = (
        P("seq", "head"),
        P("seq", "head"),
        P("seq", "head"),
        P("seq", "head"),
        P("seq", "head"),
        P("seq", "head"),
        P("seq", "head"),
        P("head"),
        P("seq", "head"),
    )
    return jax.shard_map(
        on_device,
        mesh=mesh,
        in_specs=placed,
        out_specs=(P("seq", "head"), P("seq", "head")),
        check_vma=False,
    )
```

profile of v0, /device:TPU:2, one launch (start us, length us, event | category | flops | bytes accessed | tf_op | source)
XLA Modules:
  0.0 390.9 jit_solution(8764286394529594663)
XLA Ops:
  7.2 0.7 reshape.72
  8.0 1.2 reduce-window.6
  9.2 0.1 slice.23
  9.2 0.1 copy.57
  9.4 0.1 copy.58
  9.5 0.1 add_bitcast_fusion
  9.6 0.2 slice_reduce_fusion
  9.8 0.1 bitcast_exponential_fusion
  9.8 1.1 copy.73
  10.9 2.0 convolution_add_fusion.1
  13.0 0.0 all-gather.10.cloned.1.call-start
  13.1 0.7 all-gather.10.cloned.1.call-update
  13.8 44.7 %all-gather.1 = f32[64,1,4]{2,1,0:T(1,128)S(1)} all-gather(f32[1,1,4]{2,1,0:T(1,128)S(1)} %bitcast.97), channel_id=1, replica_groups=mesh['seq'=64,'head'=8] {'seq'}, dimensions={0}, use_global_device_ids=true | all-gather | bytes 1040 | tf_op jit(solution)/shard_map/all_gather | solution.py:11
  58.6 0.4 fusion.2
  59.0 0.4 convolution_multiply_fusion
  59.4 63.1 %all-gather.16.cloned.1.call-done = f32[256,128,128]{2,1,0:T(8,128)} async-done(((f32[4,128,128]{2,1,0:T(8,128)}), f32[256,128,128]{2,1,0:T(8,128)}) %all-gather.16.cloned.1.call-update) | async-done | bytes 16777232 | tf_op jit(solution)/shard_map/all_gather | solution.py:11
  122.5 17.8 %while.3 = (s32[]{:T(128)}, f32[4,128,128]{2,1,0:T(8,128)S(1)}, s32[]{:T(128)}, f32[64,4]{1,0:T(8,128)S(1)}, f32[64,4,128,128]{3,2,1,0:T(8,128)}, /*index=5*/s32[]{:T(128)}, s32[]{:T(128)}, s32[]{:T(128)}) while((s32[]{:T(128)}, f32[4,128,128]{2,1,0:T(8,128)S(1)}, s32[]{:T(128)}, f32[64,4]{1,0:T(8,128)S(1)}, f32[64,4,128,128]{3,2,1,0:T(8,128)}, ...), condition=%wide.region_3.4_spmd, body=%wide.region_2.3_spmd.sunk | while | flops 131077 | bytes 786607 | solution.py:19
  122.6 1.1 bitcast_add_fusion.2
  123.7 1.1 bitcast_add_fusion.2
  124.8 1.1 bitcast_add_fusion.2
  125.9 1.1 bitcast_add_fusion.2
  127.0 1.1 bitcast_add_fusion.2
  128.1 1.1 bitcast_add_fusion.2
  129.2 1.1 bitcast_add_fusion.2
  130.4 1.1 bitcast_add_fusion.2
  131.5 1.1 bitcast_add_fusion.2
  132.6 1.1 bitcast_add_fusion.2
  133.7 1.1 bitcast_add_fusion.2
  134.8 1.1 bitcast_add_fusion.2
  135.9 1.1 bitcast_add_fusion.2
  137.0 1.1 bitcast_add_fusion.2
  138.1 1.1 bitcast_add_fusion.2
  139.2 1.1 bitcast_add_fusion.2
  140.3 0.4 fusion.3
  140.8 0.8 multiply_reduce_fusion.1
  141.6 0.2 copy.66
  141.8 0.9 fusion.12
  142.8 0.5 all-gather.14.cloned.1.call-update
  143.4 64.4 %all-gather.10.cloned.1.call-done = bf16[4096,512]{1,0:T(8,128)(2,1)} async-done(((bf16[64,512]{1,0:T(8,128)(2,1)}), bf16[4096,512]{1,0:T(8,128)(2,1)}) %all-gather.10.cloned.1.call-update) | async-done | bytes 4194320 | tf_op jit(solution)/shard_map/all_gather | solution.py:93
  207.8 43.4 %all-gather.8.cloned.1.call-done = bf16[256,4096]{1,0:T(8,128)(2,1)} async-done(((bf16[256,512]{1,0:T(8,128)(2,1)}), bf16[256,4096]{1,0:T(8,128)(2,1)}) %all-gather.8.cloned.1.call-update) | async-done | bytes 2097168 | tf_op jit(solution)/shard_map/all_gather | solution.py:91
  251.2 4.2 %multiply_reduce_fusion = (f32[256]{0:T(256)S(1)}, f32[256,512]{1,0:T(8,128)S(1)}) fusion(bf16[256,4096]{1,0:T(8,128)(2,1)} %all-gather.8.cloned.1.call-done, bf16[4096,512]{1,0:T(8,128)(2,1)} %all-gather.10.cloned.1.call-done, bf16[256,512]{1,0:T(8,128)(2,1)S(1)} %copy-done.4), kind=kOutput, calls=%fused_computation.22 | convolution fusion | flops 1074528000 | bytes 7078912 | tf_op jit(solution)/shard_map/dot_general | solution.py:96
  255.3 16.2 %psum.7 = f32[256]{0:T(256)S(1)} all-reduce(f32[256]{0:T(256)S(1)} %get-tuple-element.97), channel_id=1, replica_groups=mesh['seq'=64,'head'=8] {'head'}, use_global_device_ids=true, to_apply=%region_6.7 | all-reduce | flops 256 | bytes 2048 | tf_op jit(solution)/shard_map/psum | solution.py:99
  271.6 0.8 multiply_convert_fusion
  272.4 63.8 %all-gather.14.cloned.1.call-done = bf16[4096,256]{1,0:T(8,128)(2,1)} async-done(((bf16[64,256]{1,0:T(8,128)(2,1)}), bf16[4096,256]{1,0:T(8,128)(2,1)}) %all-gather.14.cloned.1.call-update) | async-done | bytes 2097168 | tf_op jit(solution)/shard_map/all_gather | solution.py:94
  336.2 43.6 %all-gather.12.cloned.1.call-done = bf16[256,4096]{1,0:T(8,128)(2,1)} async-done(((bf16[256,512]{1,0:T(8,128)(2,1)}), bf16[256,4096]{1,0:T(8,128)(2,1)}) %all-gather.12.cloned.1.call-update) | async-done | bytes 2097168 | tf_op jit(solution)/shard_map/all_gather | solution.py:103
  379.8 3.1 convolution_convert_fusion
  382.9 0.7 copy.71
  383.7 0.7 copy.72
  (44 shorter events, 0.6 us)
Async XLA Ops:
  7.2 51.4 %copy-start = (bf16[256,512]{1,0:T(8,128)(2,1)S(1)}, bf16[256,512]{1,0:T(8,128)(2,1)}, u32[]{:S(2)}) copy-start(bf16[256,512]{1,0:T(8,128)(2,1)} %param.11) | copy-start | bytes 786436
  7.2 115.3 %all-gather.16.cloned.1.call-start = ((), (), s32[]{:S(2)}) async-start(), calls=%async_computation.4 | async-start | bytes 17039360 | tf_op jit(solution)/shard_map/all_gather | solution.py:11
  13.0 194.8 %all-gather.10.cloned.1.call-start = ((), (), s32[]{:S(2)}) async-start(), calls=%async_computation.1 | async-start | bytes 4259840 | tf_op jit(solution)/shard_map/all_gather | solution.py:93
  13.8 237.4 %all-gather.8.cloned.1.call-start = ((), (), s32[]{:S(2)}) async-start(), calls=%async_computation | async-start | bytes 2359296 | tf_op jit(solution)/shard_map/all_gather | solution.py:91
  122.5 18.2 %copy-start.1 = (bf16[256,512]{1,0:T(8,128)(2,1)S(1)}, bf16[256,512]{1,0:T(8,128)(2,1)}, u32[]{:S(2)}) copy-start(bf16[256,512]{1,0:T(8,128)(2,1)} %param.13) | copy-start | bytes 786436
  140.8 1.1 copy-start.2
  141.5 1.8 copy-start.3
  141.5 109.7 %copy-start.4 = (bf16[256,512]{1,0:T(8,128)(2,1)S(1)}, bf16[256,512]{1,0:T(8,128)(2,1)}, u32[]{:S(2)}) copy-start(bf16[256,512]{1,0:T(8,128)(2,1)} %param.15) | copy-start | bytes 786436
  142.7 193.4 %all-gather.14.cloned.1.call-start = ((), (), s32[]{:S(2)}) async-start(), calls=%async_computation.3 | async-start | bytes 2129920 | tf_op jit(solution)/shard_map/all_gather | solution.py:94
  143.3 236.5 %all-gather.12.cloned.1.call-start = ((), (), s32[]{:S(2)}) async-start(), calls=%async_computation.2 | async-start | bytes 2359296 | tf_op jit(solution)/shard_map/all_gather | solution.py:103
Sparse Core Ops, SparseCore 0:
  13.1 109.3 all-gather.15
  125.8 81.8 all-gather.9
  209.9 41.2 all-gather.7
  254.4 81.7 all-gather.13
  338.1 41.6 all-gather.11
where the time goes:
time: 393 us; the launch traced here: 391 us
  waiting for transfers between devices  280 us (71%)
  blocking collectives  60.9 us (15%)
  other arithmetic  20.2 us (5%)
  between operations  14 us (4%)
  matrix products  11.3 us (3%)
  local copies, waits for them, and re-layouts  4.19 us (1%)
    all_gather x1, waiting for transfers between devices, on_device(): lax.all_gather(out_weight, 'seq', axis=0, tiled=True)  64.4 us
    all_gather x1, waiting for transfers between devices, on_device(): lax.all_gather(kv_weight, 'seq', axis=0, tiled=True)  63.8 us
    all_gather x1, waiting for transfers between devices, entering(): gathered = jax.tree.map(lambda a: lax.all_gather(a, axis), part)  63.1 us
    all_gather x1, blocking collectives, entering(): gathered = jax.tree.map(lambda a: lax.all_gather(a, axis), part)  44.7 us
    all_gather x1, waiting for transfers between devices, on_device(): normalized = lax.all_gather(local_norm, 'head', axis=1, tiled=True)  43.6 us
    all_gather x1, waiting for transfers between devices, on_device(): all_heads = lax.all_gather(mixed, 'head', axis=1, tiled=True)  43.4 us
    add x16, other arithmetic, combine_states(): later[0][:, None, None] * earlier[1] + later[1]  17 us
    psum x1, blocking collectives, on_device(): squares = lax.psum(jnp.sum(wide * wide, axis=1), 'head')  16.2 us
  transfers between devices with their start and end apart: 5, of which 5 were waited for; matrix products, arithmetic and copies ran while one was open for 6% of the time, Pallas kernels for 0%

commit v1 on v0

--- a/solution.py
+++ b/solution.py
@@ -100,7 +100,23 @@
     features = wide.shape[1] * lax.axis_size("head")
     inverse = lax.rsqrt(squares[:, None] / features + 1e-06)
     local_norm = (wide * inverse * norm_gain.astype(jnp.float32)[None, :]).astype(jnp.bfloat16)
-    normalized = lax.all_gather(local_norm, "head", axis=1, tiled=True)
+    ways, here, turn = (lax.axis_size("head"), lax.axis_index("head"), local_norm.shape[1])
+    shape = [n * ways if d == 1 else n for d, n in enumerate(local_norm.shape)]
+    full = lax.dynamic_update_slice_in_dim(
+        jnp.zeros(shape, local_norm.dtype), local_norm, here * turn, axis=1
+    )
+    going_up = going_down = local_norm
+    for far in range(1, ways // 2 + 1):
+        going_up = lax.ppermute(going_up, "head", [(d, (d + 1) % ways) for d in range(ways)])
+        full = lax.dynamic_update_slice_in_dim(full, going_up, (here - far) % ways * turn, axis=1)
+        if 2 * far < ways:
+            going_down = lax.ppermute(
+                going_down, "head", [(d, (d - 1) % ways) for d in range(ways)]
+            )
+            full = lax.dynamic_update_slice_in_dim(
+                full, going_down, (here + far) % ways * turn, axis=1
+            )
+    normalized = full
     projected = jnp.dot(normalized, kv_full, preferred_element_type=jnp.float32)
     cache_heads = kv_weight.shape[1] // (2 * width)
     arranged = projected.reshape(tokens, cache_heads, 2, width)

time: 393 us -> 351 us (0.89)
  the two profiles are of different devices: /device:TPU:2 before, /device:TPU:1 now
where the time goes in v1:
time: 351 us; the launch traced here: 349 us
  waiting for transfers between devices  235 us (67%)
  blocking collectives  58.4 us (17%)
  starting transfers between devices  22.2 us (6%)
  between operations  14.2 us (4%)
  matrix products  10.7 us (3%)
  local copies, waits for them, and re-layouts  4.46 us (1%)
  other arithmetic  3.56 us (1%)
    all_gather x1, waiting for transfers between devices, on_device(): lax.all_gather(out_weight, 'seq', axis=0, tiled=True)  80.9 us
    all_gather x1, waiting for transfers between devices, entering(): gathered = jax.tree.map(lambda a: lax.all_gather(a, axis), part)  64 us
    all_gather x1, blocking collectives, entering(): gathered = jax.tree.map(lambda a: lax.all_gather(a, axis), part)  46.4 us
    all_gather x1, waiting for transfers between devices, on_device(): all_heads = lax.all_gather(mixed, 'head', axis=1, tiled=True)  38.3 us
    all_gather x1, waiting for transfers between devices, on_device(): lax.all_gather(kv_weight, 'seq', axis=0, tiled=True)  35.6 us
    ppermute x4, waiting for transfers between devices, on_device(): lax.ppermute(going_up, 'head', [(d, (d + 1) % ways) for d in range(ways)])  15.3 us
    ppermute x3, starting transfers between devices, on_device(): lax.ppermute(going_down, 'head', [(d, (d - 1) % ways) for d in range(ways)])  14.3 us
    psum x1, blocking collectives, on_device(): squares = lax.psum(jnp.sum(wide * wide, axis=1), 'head')  12 us
  transfers between devices with their start and end apart: 11, of which 8 were waited for; matrix products, arithmetic and copies ran while one was open for 3% of the time, Pallas kernels for 0%

profile of v1, /device:TPU:1, one launch (start us, length us, event | category | flops | bytes accessed | tf_op | source)
XLA Modules:
  0.0 348.8 jit_solution(12634482392994203355)
XLA Ops:
  7.2 0.0 all-gather.13.cloned.1.call-start
  7.2 0.7 reshape.72
  8.0 1.2 reduce-window.6
  9.2 0.1 slice.23
  9.2 0.1 copy.57
  9.4 0.1 copy.58
  9.5 0.1 add_bitcast_fusion
  9.6 0.2 slice_reduce_fusion
  9.8 0.1 bitcast_exponential_fusion
  9.8 1.1 copy.73
  10.9 2.0 convolution_add_fusion.1
  13.0 0.0 all-gather.9.cloned.1.call-start
  13.1 0.7 all-gather.9.cloned.1.call-update
  13.8 0.0 all-gather.7.cloned.1.call-start
  13.8 46.4 %all-gather.1 = f32[64,1,4]{2,1,0:T(1,128)S(1)} all-gather(f32[1,1,4]{2,1,0:T(1,128)S(1)} %bitcast.97), channel_id=1, replica_groups=mesh['seq'=64,'head'=8] {'seq'}, dimensions={0}, use_global_device_ids=true | all-gather | bytes 1040 | tf_op jit(solution)/shard_map/all_gather | solution.py:11
  60.2 0.4 fusion.2
  60.6 0.4 convolution_multiply_fusion
  61.0 64.0 %all-gather.13.cloned.1.call-done = f32[256,128,128]{2,1,0:T(8,128)} async-done(((f32[4,128,128]{2,1,0:T(8,128)}), f32[256,128,128]{2,1,0:T(8,128)}) %all-gather.13.cloned.1.call-update) | async-done | bytes 16777232 | tf_op jit(solution)/shard_map/all_gather | solution.py:11
  125.0 1.1 while.3
  125.1 1.1 bitcast_add_fusion.2
  126.2 0.4 fusion.3
  126.7 0.8 multiply_reduce_fusion.1
  127.5 0.2 copy.66
  127.7 0.9 fusion.12
  128.6 0.0 all-gather.7.cloned.1.call-update
  128.6 0.0 all-gather.11.cloned.1.call-start
  128.7 0.5 all-gather.11.cloned.1.call-update
  129.2 80.9 %all-gather.9.cloned.1.call-done = bf16[4096,512]{1,0:T(8,128)(2,1)} async-done(((bf16[64,512]{1,0:T(8,128)(2,1)}), bf16[4096,512]{1,0:T(8,128)(2,1)}) %all-gather.9.cloned.1.call-update) | async-done | bytes 4194320 | tf_op jit(solution)/shard_map/all_gather | solution.py:93
  210.1 38.3 %all-gather.7.cloned.1.call-done = bf16[256,4096]{1,0:T(8,128)(2,1)} async-done(((bf16[256,512]{1,0:T(8,128)(2,1)}), bf16[256,4096]{1,0:T(8,128)(2,1)}) %all-gather.7.cloned.1.call-update) | async-done | bytes 2097168 | tf_op jit(solution)/shard_map/all_gather | solution.py:91
  248.4 4.2 %multiply_reduce_fusion = (f32[256]{0:T(256)S(1)}, f32[256,512]{1,0:T(8,128)S(1)}) fusion(bf16[256,4096]{1,0:T(8,128)(2,1)} %all-gather.7.cloned.1.call-done, bf16[4096,512]{1,0:T(8,128)(2,1)} %all-gather.9.cloned.1.call-done, bf16[256,512]{1,0:T(8,128)(2,1)S(1)} %copy-done.4), kind=kOutput, calls=%fused_computation.22 | convolution fusion | flops 1074528000 | bytes 7078912 | tf_op jit(solution)/shard_map/dot_general | solution.py:96
  252.5 12.0 %psum.7 = f32[256]{0:T(256)S(1)} all-reduce(f32[256]{0:T(256)S(1)} %get-tuple-element.99), channel_id=1, replica_groups=mesh['seq'=64,'head'=8] {'head'}, use_global_device_ids=true, to_apply=%region_6.7 | all-reduce | flops 256 | bytes 2048 | tf_op jit(solution)/shard_map/psum | solution.py:99
  264.5 0.2 broadcast_in_dim.56
  264.8 0.1 constant_dynamic-update-slice_fusion.7
  264.9 2.0 collective-permute-start
  266.9 4.5 %collective-permute-start.1 = (bf16[256,512]{1,0:T(8,128)(2,1)S(1)}, bf16[256,512]{1,0:T(8,128)(2,1)S(1)}, u32[]{:S(2)}, u32[]{:S(2)}) collective-permute-start(bf16[256,512]{1,0:T(8,128)(2,1)S(1)} %get-tuple-element.90), channel_id=1, source_target_pairs={{0,7},{1,0},{2,1},{3,2},{4,3},{5,4},{6,5},{7,6},{8,15},{9,8},{10,9... | collective-permute-start | bytes 786440 | tf_op jit(solution)/shard_map/ppermute | solution.py:113
  271.4 1.9 collective-permute-done
  273.3 1.9 collective-permute-start.2
  275.2 4.9 %collective-permute-start.3 = (bf16[256,512]{1,0:T(8,128)(2,1)S(1)}, bf16[256,512]{1,0:T(8,128)(2,1)S(1)}, u32[]{:S(2)}, u32[]{:S(2)}) collective-permute-start(bf16[256,512]{1,0:T(8,128)(2,1)S(1)} %collective-permute-done.1), channel_id=1, source_target_pairs={{0,7},{1,0},{2,1},{3,2},{4,3},{5,4},{6,5},{7,6},{8,15},{9,8},{10,9... | collective-permute-start | bytes 786440 | tf_op jit(solution)/shard_map/ppermute | solution.py:113
  280.3 3.7 %collective-permute-done.2 = bf16[256,512]{1,0:T(8,128)(2,1)S(1)} collective-permute-done((bf16[256,512]{1,0:T(8,128)(2,1)S(1)}, bf16[256,512]{1,0:T(8,128)(2,1)S(1)}, u32[]{:S(2)}, u32[]{:S(2)}) %collective-permute-start.2) | collective-permute-done | bytes 262176 | tf_op jit(solution)/shard_map/ppermute | solution.py:110
  284.0 1.9 collective-permute-start.4
  286.0 4.9 %collective-permute-start.5 = (bf16[256,512]{1,0:T(8,128)(2,1)S(1)}, bf16[256,512]{1,0:T(8,128)(2,1)S(1)}, u32[]{:S(2)}, u32[]{:S(2)}) collective-permute-start(bf16[256,512]{1,0:T(8,128)(2,1)S(1)} %collective-permute-done.3), channel_id=1, source_target_pairs={{0,7},{1,0},{2,1},{3,2},{4,3},{5,4},{6,5},{7,6},{8,15},{9,8},{10,9... | collective-permute-start | bytes 786440 | tf_op jit(solution)/shard_map/ppermute | solution.py:113
  291.0 2.8 collective-permute-done.4
  293.8 1.9 collective-permute-start.6
  295.8 6.8 %collective-permute-done.6 = bf16[256,512]{1,0:T(8,128)(2,1)S(1)} collective-permute-done((bf16[256,512]{1,0:T(8,128)(2,1)S(1)}, bf16[256,512]{1,0:T(8,128)(2,1)S(1)}, u32[]{:S(2)}, u32[]{:S(2)}) %collective-permute-start.6) | collective-permute-done | bytes 262176 | tf_op jit(solution)/shard_map/ppermute | solution.py:110
  302.7 35.6 %all-gather.11.cloned.1.call-done = bf16[4096,256]{1,0:T(8,128)(2,1)} async-done(((bf16[64,256]{1,0:T(8,128)(2,1)}), bf16[4096,256]{1,0:T(8,128)(2,1)}) %all-gather.11.cloned.1.call-update) | async-done | bytes 2097168 | tf_op jit(solution)/shard_map/all_gather | solution.py:94
  338.3 2.5 convolution_convert_fusion
  340.8 0.7 copy.71
  341.6 0.7 copy.72
  (33 shorter events, 0.4 us)
Async XLA Ops:
  7.2 53.0 %copy-start = (bf16[256,512]{1,0:T(8,128)(2,1)S(1)}, bf16[256,512]{1,0:T(8,128)(2,1)}, u32[]{:S(2)}) copy-start(bf16[256,512]{1,0:T(8,128)(2,1)} %param.11) | copy-start | bytes 786436
  7.2 117.8 %all-gather.13.cloned.1.call-start = ((), (), s32[]{:S(2)}) async-start(), calls=%async_computation.3 | async-start | bytes 17039360 | tf_op jit(solution)/shard_map/all_gather | solution.py:11
  13.0 197.1 %all-gather.9.cloned.1.call-start = ((), (), s32[]{:S(2)}) async-start(), calls=%async_computation.1 | async-start | bytes 4259840 | tf_op jit(solution)/shard_map/all_gather | solution.py:93
  13.8 234.6 %all-gather.7.cloned.1.call-start = ((), (), s32[]{:S(2)}) async-start(), calls=%async_computation | async-start | bytes 2359296 | tf_op jit(solution)/shard_map/all_gather | solution.py:91
  125.0 1.6 copy-start.1
  126.6 1.1 copy-start.2
  127.4 1.8 copy-start.3
  127.4 120.9 %copy-start.4 = (bf16[256,512]{1,0:T(8,128)(2,1)S(1)}, bf16[256,512]{1,0:T(8,128)(2,1)}, u32[]{:S(2)}) copy-start(bf16[256,512]{1,0:T(8,128)(2,1)} %param.15) | copy-start | bytes 786436
  128.6 209.7 %all-gather.11.cloned.1.call-start = ((), (), s32[]{:S(2)}) async-start(), calls=%async_computation.2 | async-start | bytes 2129920 | tf_op jit(solution)/shard_map/all_gather | solution.py:94
  264.9 8.4 %collective-permute-start = (bf16[256,512]{1,0:T(8,128)(2,1)S(1)}, bf16[256,512]{1,0:T(8,128)(2,1)S(1)}, u32[]{:S(2)}, u32[]{:S(2)}) collective-permute-start(bf16[256,512]{1,0:T(8,128)(2,1)S(1)} %get-tuple-element.90), channel_id=1, source_target_pairs={{0,1},{1,2},{2,3},{3,4},{4,5},{5,6},{6,7},{7,0},{8,9},{9,10},{10,1... | collective-permute-start | bytes 786440 | tf_op jit(solution)/shard_map/ppermute | solution.py:110
  266.9 8.3 %collective-permute-start.1 = (bf16[256,512]{1,0:T(8,128)(2,1)S(1)}, bf16[256,512]{1,0:T(8,128)(2,1)S(1)}, u32[]{:S(2)}, u32[]{:S(2)}) collective-permute-start(bf16[256,512]{1,0:T(8,128)(2,1)S(1)} %get-tuple-element.90), channel_id=1, source_target_pairs={{0,7},{1,0},{2,1},{3,2},{4,3},{5,4},{6,5},{7,6},{8,15},{9,8},{10,9... | collective-permute-start | bytes 786440 | tf_op jit(solution)/shard_map/ppermute | solution.py:113
  273.3 10.7 %collective-permute-start.2 = (bf16[256,512]{1,0:T(8,128)(2,1)S(1)}, bf16[256,512]{1,0:T(8,128)(2,1)S(1)}, u32[]{:S(2)}, u32[]{:S(2)}) collective-permute-start(bf16[256,512]{1,0:T(8,128)(2,1)S(1)} %collective-permute-done), channel_id=1, source_target_pairs={{0,1},{1,2},{2,3},{3,4},{4,5},{5,6},{6,7},{7,0},{8,9},{9,10},{10,1... | collective-permute-start | bytes 786440 | tf_op jit(solution)/shard_map/ppermute | solution.py:110
  275.2 10.8 %collective-permute-start.3 = (bf16[256,512]{1,0:T(8,128)(2,1)S(1)}, bf16[256,512]{1,0:T(8,128)(2,1)S(1)}, u32[]{:S(2)}, u32[]{:S(2)}) collective-permute-start(bf16[256,512]{1,0:T(8,128)(2,1)S(1)} %collective-permute-done.1), channel_id=1, source_target_pairs={{0,7},{1,0},{2,1},{3,2},{4,3},{5,4},{6,5},{7,6},{8,15},{9,8},{10,9... | collective-permute-start | bytes 786440 | tf_op jit(solution)/shard_map/ppermute | solution.py:113
  284.0 9.8 %collective-permute-start.4 = (bf16[256,512]{1,0:T(8,128)(2,1)S(1)}, bf16[256,512]{1,0:T(8,128)(2,1)S(1)}, u32[]{:S(2)}, u32[]{:S(2)}) collective-permute-start(bf16[256,512]{1,0:T(8,128)(2,1)S(1)} %collective-permute-done.2), channel_id=1, source_target_pairs={{0,1},{1,2},{2,3},{3,4},{4,5},{5,6},{6,7},{7,0},{8,9},{9,10},{10,1... | collective-permute-start | bytes 786440 | tf_op jit(solution)/shard_map/ppermute | solution.py:110
  286.0 9.8 %collective-permute-start.5 = (bf16[256,512]{1,0:T(8,128)(2,1)S(1)}, bf16[256,512]{1,0:T(8,128)(2,1)S(1)}, u32[]{:S(2)}, u32[]{:S(2)}) collective-permute-start(bf16[256,512]{1,0:T(8,128)(2,1)S(1)} %collective-permute-done.3), channel_id=1, source_target_pairs={{0,7},{1,0},{2,1},{3,2},{4,3},{5,4},{6,5},{7,6},{8,15},{9,8},{10,9... | collective-permute-start | bytes 786440 | tf_op jit(solution)/shard_map/ppermute | solution.py:113
  293.8 8.9 %collective-permute-start.6 = (bf16[256,512]{1,0:T(8,128)(2,1)S(1)}, bf16[256,512]{1,0:T(8,128)(2,1)S(1)}, u32[]{:S(2)}, u32[]{:S(2)}) collective-permute-start(bf16[256,512]{1,0:T(8,128)(2,1)S(1)} %collective-permute-done.4), channel_id=1, source_target_pairs={{0,1},{1,2},{2,3},{3,4},{4,5},{5,6},{6,7},{7,0},{8,9},{9,10},{10,1... | collective-permute-start | bytes 786440 | tf_op jit(solution)/shard_map/ppermute | solution.py:110
Sparse Core Ops, SparseCore 0:
  13.1 111.8 all-gather.12
  128.4 81.6 all-gather.8
  212.2 36.1 all-gather.6
  251.6 86.6 all-gather.10
